TPU v7x, 32 devices: a whole 2x2x4 slice. The times are simulated.
32 devices in a mesh: layer: 2 (over core), feat: 4 (over y, x), seq: 4 (over z).
Axes of the slice: x: 2, y: 2, z: 4, core: 2. Of those that a mesh axis runs over, the one named last changes fastest.
Arguments:
- mlp_inputs: bfloat16 [2, 768, 2304], P('layer', 'seq'), may hold values from -6 to 6
- enc_weight: bfloat16 [2, 2304, 4096], P('layer', 'seq', 'feat'), may hold values from -0.125 to 0.125
- enc_bias: float32 [2, 4096], P('layer', 'feat'), may hold values from -3 to 3
- dec_weight: bfloat16 [2, 4096, 2304], P('layer', 'feat', 'seq'), may hold values from -0.1875 to 0.1875
- dec_cross: bfloat16 [4096, 2304], P('feat', ('layer', 'seq')), may hold values from -0.1875 to 0.1875
- dec_bias: float32 [2, 2304], P('layer', 'feat'), may hold values from -3 to 3
Outputs:
- recon: bfloat16 [2, 768, 2304], P('layer', 'seq', 'feat')
All inputs are finite; a program needn't handle non-finite values.
Results may differ from a plain program's by a relative error of at most 0.0047.
Values may be sent and summed in bfloat16 or wider, within the bound.
A program may use at most 64 MiB of HBM per device.

v0:
```python
import jax
import jax.numpy as jnp
from jax import lax
from jax.sharding import PartitionSpec as P


def passed_along(x, axis, by):
    devices = lax.axis_size(axis)
    pairs = [(i, i + by) for i in range(devices) if 0 <= i + by < devices]
    return lax.ppermute(x, axis, pairs)


def per_device(mlp_inputs, enc_weight, enc_bias, dec_weight, dec_cross, dec_bias):
    token_rows = mlp_inputs[0]
    layer_index = lax.axis_index("layer")
    pre_acts = jnp.dot(
        token_rows,
        lax.all_gather(enc_weight[0], "seq", axis=0, tiled=True),
        preferred_element_type=jnp.float32,
    )
    features = jnp.maximum(pre_acts + enc_bias[0], 0.0).astype(jnp.bfloat16)
    own_terms = jnp.dot(
        features,
        lax.all_gather(dec_weight[0], "seq", axis=1, tiled=True),
        preferred_element_type=jnp.float32,
    )
    half_rows = features.shape[0] // 2
    sent_half = passed_along(features[half_rows:], "layer", 1)
    cross_input = jnp.where(layer_index == 0, features[:half_rows], sent_half)
    cross_terms = jnp.dot(
        cross_input,
        lax.all_gather(dec_cross, ("layer", "seq"), axis=1, tiled=True),
        preferred_element_type=jnp.float32,
    )
    own_sums, cross_sums = (
        lax.psum_scatter(own_terms, "feat", scatter_dimension=1, tiled=True),
        lax.psum_scatter(cross_terms, "feat", scatter_dimension=1, tiled=True),
    )
    moved_sums = passed_along(cross_sums, "layer", 1)
    cross_full = jnp.concatenate([moved_sums, cross_sums], axis=0)
    total = own_sums + dec_bias[0] + jnp.where(layer_index == 1, cross_full, 0.0)
    return total.astype(jnp.bfloat16)[None]


def solution(mesh):
    placed = (
        P("layer", "seq", None),
        P("layer", "seq", "feat"),
        P("layer", "feat"),
        P("layer", "feat", "seq"),
        P("feat", ("layer", "seq")),
        P("layer", "feat"),
    )
    return jax.shard_map(
        per_device, mesh=mesh, in_specs=placed, out_specs=P("layer", "seq", "feat"), check_vma=False
    )
```

profile of v0, /device:TPU:0, one launch (start us, length us, event | category | flops | bytes accessed | tf_op | source)
XLA Modules:
  0.0 320.9 jit_solution(13372327382899990657)
XLA Ops:
  6.5 0.0 copy-start
  6.5 0.0 all-gather.8.cloned.1.call-start
  6.5 0.7 all-gather.8.cloned.1.call-update
  7.3 0.0 all-gather.6.cloned.1.call-start
  7.3 0.7 all-gather.6.cloned.1.call-update
  8.0 0.0 all-gather.10.cloned.1.call-start
  8.1 0.7 all-gather.10.cloned.1.call-update
  8.7 0.0 reduce-scatter.9.cloned.1.call-start
  8.8 92.3 %all-gather.8.cloned.1.call-done = bf16[1,2304,1024]{2,1,0:T(8,128)(2,1)} async-done(((bf16[1,576,1024]{2,1,0:T(8,128)(2,1)}), bf16[1,2304,1024]{2,1,0:T(8,128)(2,1)}) %all-gather.8.cloned.1.call-update) | async-done | bytes 4718608 | tf_op jit(solution)/shard_map/all_gather | solution.py:18
  101.0 0.0 copy-done
  101.0 3.4 %fusion.13 = bf16[192,1024]{1,0:T(8,128)(2,1)S(1)} fusion(bf16[1,2304,1024]{2,1,0:T(8,128)(2,1)} %all-gather.8.cloned.1.call-done, bf16[1,192,2304]{2,1,0:T(8,128)(2,1)S(1)} %copy-done, f32[1024]{0:T(1024)} %bitcast.30), kind=kOutput, calls=%fused_computation.8 | convolution fusion | flops 906559488 | bytes 6000640 | tf_op jit(solution)/shard_map/dot_general | solution.py:16
  104.5 1.7 collective-permute-start
  106.2 1.0 collective-permute-done
  107.2 45.0 %all-gather.6.cloned.1.call-done = bf16[1024,2304]{0,1:T(8,128)(2,1)} async-done(((bf16[1024,288]{0,1:T(8,128)(2,1)}), bf16[1024,2304]{0,1:T(8,128)(2,1)}) %all-gather.6.cloned.1.call-update) | async-done | bytes 4718608 | tf_op jit(solution)/shard_map/all_gather | solution.py:32
  152.3 4.7 %convolution_bitcast_fusion = f32[2304,96]{1,0:T(8,128)} fusion(bf16[1024,2304]{0,1:T(8,128)(2,1)} %all-gather.6.cloned.1.call-done, bf16[96,1024]{1,0:T(8,128)(2,1)S(1)} %collective-permute-done, bf16[192,1024]{1,0:T(8,128)(2,1)S(1)} %fusion.13, pred[]{:T(512)S(6)} %eq.7), kind=kOutput, calls=%fused_computation.5 | convolution fusion | flops 453083136 | bytes 5996545
  157.0 0.0 reduce-scatter.9.cloned.1.call-update
  157.1 0.0 copy-start.1
  157.1 0.0 reduce-scatter.7.cloned.1.call-start
  157.1 84.9 %all-gather.10.cloned.1.call-done = bf16[1,1024,2304]{1,2,0:T(8,128)(2,1)} async-done(((bf16[1,1024,576]{1,2,0:T(8,128)(2,1)}), bf16[1,1024,2304]{1,2,0:T(8,128)(2,1)}) %all-gather.10.cloned.1.call-update) | async-done | bytes 4718608 | tf_op jit(solution)/shard_map/all_gather | solution.py:24
  242.0 5.2 %fusion.4 = f32[2304,192]{1,0:T(8,128)} fusion(bf16[192,1024]{1,0:T(8,128)(2,1)S(1)} %fusion.13, bf16[1,1024,2304]{1,2,0:T(8,128)(2,1)} %all-gather.10.cloned.1.call-done), kind=kOutput, calls=%fused_computation.4 | convolution fusion | flops 905969664 | bytes 6881280
  247.2 0.0 reduce-scatter.7.cloned.1.call-update
  247.2 24.7 %reduce-scatter.9.cloned.1.call-done = f32[576,96]{1,0:T(8,128)} async-done(((f32[2304,96]{1,0:T(8,128)}), f32[576,96]{1,0:T(8,128)}) %reduce-scatter.9.cloned.1.call-update) | async-done | bytes 221200
  272.0 1.1 copy.10
  273.1 1.6 collective-permute-start.1
  274.7 0.0 copy-done.1
  274.7 37.5 %reduce-scatter.7.cloned.1.call-done = f32[576,192]{1,0:T(8,128)} async-done(((f32[2304,192]{1,0:T(8,128)}), f32[576,192]{1,0:T(8,128)}) %reduce-scatter.7.cloned.1.call-update) | async-done | bytes 442384
  312.3 1.3 copy.8
  313.6 0.0 collective-permute-done.1
  313.6 0.8 fusion.19
  (2 shorter events, 0.0 us)
Async XLA Ops:
  6.5 94.5 %copy-start = (bf16[1,192,2304]{2,1,0:T(8,128)(2,1)S(1)}, bf16[1,192,2304]{2,1,0:T(8,128)(2,1)}, u32[]{:S(2)}) copy-start(bf16[1,192,2304]{2,1,0:T(8,128)(2,1)} %param.6) | copy-start | bytes 2654212
  6.5 94.5 %all-gather.8.cloned.1.call-start = ((), (), s32[]{:S(2)}) async-start(), calls=%async_computation.3 | async-start | bytes 5898240 | tf_op jit(solution)/shard_map/all_gather | solution.py:18
  7.3 145.0 %all-gather.6.cloned.1.call-start = ((), (), s32[]{:S(2)}) async-start(), calls=%async_computation.2 | async-start | bytes 5308416 | tf_op jit(solution)/shard_map/all_gather | solution.py:32
  8.0 234.0 %all-gather.10.cloned.1.call-start = ((), (), s32[]{:S(2)}) async-start(), calls=%async_computation.4 | async-start | bytes 5898240 | tf_op jit(solution)/shard_map/all_gather | solution.py:24
  8.7 263.2 %reduce-scatter.9.cloned.1.call-start = ((), (), s32[]{:S(2)}) async-start(), calls=%async_computation.6 | async-start | bytes 1474560
  104.5 2.7 collective-permute-start
  157.1 117.6 %copy-start.1 = (f32[1,576]{1,0:T(1,128)S(1)}, f32[1,576]{1,0:T(1,128)}, u32[]{:S(2)}) copy-start(f32[1,576]{1,0:T(1,128)} %param.11) | copy-start | bytes 6916
  157.1 155.2 %reduce-scatter.7.cloned.1.call-start = ((), (), s32[]{:S(2)}) async-start(), calls=%async_computation.5 | async-start | bytes 2949120
  273.1 40.5 %collective-permute-start.1 = (f32[96,576]{1,0:T(8,128)S(1)}, f32[96,576]{1,0:T(8,128)S(1)}, u32[]{:S(2)}, u32[]{:S(2)}) collective-permute-start(f32[96,576]{1,0:T(8,128)S(1)} %copy.10), channel_id=1, source_target_pairs={{0,16},{1,17},{2,18},{3,19},{4,20},{5,21},{6,22},{7,23},{8,24},{9,... | collective-permute-start | bytes 663560 | tf_op jit(solution)/shard_map/ppermute | solution.py:10
Sparse Core Ops, SparseCore 0:
  8.9 92.0 all-gather.7
  102.6 49.6 all-gather.5
  153.9 88.1 all-gather.9
  244.8 27.1 reduce-scatter.8
  274.9 37.3 reduce-scatter.6
where the time goes:
time: 321 us
  waiting for transfers between devices  288 us (90%)
  matrix products  13.3 us (4%)
  between operations  13.2 us (4%)
  starting transfers between devices  3.46 us (1%)
    all_gather x1, waiting for transfers between devices, per_device(): lax.all_gather(enc_weight[0], 'seq', axis=0, tiled=True)  92.3 us
    all_gather x1, waiting for transfers between devices, per_device(): lax.all_gather(dec_weight[0], 'seq', axis=1, tiled=True)  84.9 us
    unnamed x7, waiting for transfers between devices  64.4 us
    all_gather x1, waiting for transfers between devices, per_device(): lax.all_gather(dec_cross, ('layer', 'seq'), axis=1, tiled=True)  45 us
    unnamed x2, matrix products  9.92 us
  transfers between devices with their start and end apart: 7, of which 6 were waited for; matrix products, arithmetic and copies ran while one was open for 5% of the time, Pallas kernels for 0%

commit v1 on v0

--- a/solution.py
+++ b/solution.py
@@ -2,6 +2,24 @@
 import jax.numpy as jnp
 from jax import lax
 from jax.sharding import PartitionSpec as P
+
+
+def gather_around(array, axis, dim):
+    ways, here, step = (lax.axis_size(axis), lax.axis_index(axis), array.shape[dim])
+    lengths = [n * ways if d == dim else n for d, n in enumerate(array.shape)]
+    full = lax.dynamic_update_slice_in_dim(
+        jnp.zeros(lengths, array.dtype), array, here * step, axis=dim
+    )
+    going_up = going_down = array
+    for far in range(1, ways // 2 + 1):
+        going_up = lax.ppermute(going_up, axis, [(d, (d + 1) % ways) for d in range(ways)])
+        full = lax.dynamic_update_slice_in_dim(full, going_up, (here - far) % ways * step, axis=dim)
+        if 2 * far < ways:
+            going_down = lax.ppermute(going_down, axis, [(d, (d - 1) % ways) for d in range(ways)])
+            full = lax.dynamic_update_slice_in_dim(
+                full, going_down, (here + far) % ways * step, axis=dim
+            )
+    return full
 
 
 def passed_along(x, axis, by):
@@ -14,9 +32,7 @@
     token_rows = mlp_inputs[0]
     layer_index = lax.axis_index("layer")
     pre_acts = jnp.dot(
-        token_rows,
-        lax.all_gather(enc_weight[0], "seq", axis=0, tiled=True),
-        preferred_element_type=jnp.float32,
+        token_rows, gather_around(enc_weight[0], "seq", 0), preferred_element_type=jnp.float32
     )
     features = jnp.maximum(pre_acts + enc_bias[0], 0.0).astype(jnp.bfloat16)
     own_terms = jnp.dot(

time: 321 us -> 285 us (0.89)
  waiting for transfers between devices: 288 us -> 206 us
  starting transfers between devices: 3.46 us -> 46.7 us
  local copies, waits for them, and re-layouts: 2.41 us -> 6.03 us
    all_gather x1 -> x0, waiting for transfers between devices: 92.3 us -> none  [per_device(): lax.all_gather(enc_weight[0], 'seq', axis=0, tiled=True)]
    ppermute x0 -> x3, waiting for transfers between devices: none -> 82.4 us  [the longest x2 75.9 us: gather_around(): lax.ppermute(going_up, axis, [(d, (d + 1) % ways) for d in range(ways)])]
    all_gather x1, waiting for transfers between devices: 45 us -> 0.01 us  [per_device(): lax.all_gather(dec_cross, ('layer', 'seq'), axis=1, tiled=True)]
    ppermute x0 -> x3, starting transfers between devices: none -> 43.7 us  [the longest x2 41.6 us: gather_around(): lax.ppermute(going_up, axis, [(d, (d + 1) % ways) for d in range(ways)])]
    all_gather x1, waiting for transfers between devices: 84.9 us -> 58.4 us  [per_device(): lax.all_gather(dec_weight[0], 'seq', axis=1, tiled=True)]
    unnamed x7 -> x6, waiting for transfers between devices: 64.4 us -> 64.6 us
  transfers between devices with their start and end apart: 7 -> 9, of which waited for: 6 -> 7; matrix products, arithmetic and copies ran while one was open for 5% -> 6% of each run, Pallas kernels for 0% -> 0%
where the time goes in v1:
time: 285 us; the launch traced here: 284 us
  waiting for transfers between devices  206 us (72%)
  starting transfers between devices  46.7 us (16%)
  between operations  13.3 us (5%)
  matrix products  11.1 us (4%)
  local copies, waits for them, and re-layouts  6.03 us (2%)
    ppermute x2, waiting for transfers between devices, gather_around(): lax.ppermute(going_up, axis, [(d, (d + 1) % ways) for d in range(ways)])  75.9 us
    unnamed x6, waiting for transfers between devices  64.6 us
    all_gather x1, waiting for transfers between devices, per_device(): lax.all_gather(dec_weight[0], 'seq', axis=1, tiled=True)  58.4 us
    ppermute x2, starting transfers between devices, gather_around(): lax.ppermute(going_up, axis, [(d, (d + 1) % ways) for d in range(ways)])  41.6 us
    unnamed x2, matrix products  9.99 us
    ppermute x1, waiting for transfers between devices, gather_around(): lax.ppermute(going_down, axis, [(d, (d - 1) % ways) for d in range(ways)])  6.52 us
  transfers between devices with their start and end apart: 9, of which 7 were waited for; matrix products, arithmetic and copies ran while one was open for 6% of the time, Pallas kernels for 0%

profile of v1, /device:TPU:0, one launch (start us, length us, event | category | flops | bytes accessed | tf_op | source)
XLA Modules:
  0.0 284.2 jit_solution(3915319443135844136)
XLA Ops:
  6.5 0.0 copy-start
  6.5 0.0 copy-start.1
  6.5 0.0 all-gather.4.cloned.1.call-start
  6.5 0.7 all-gather.4.cloned.1.call-update
  7.3 0.0 all-gather.6.cloned.1.call-start
  7.3 0.7 all-gather.6.cloned.1.call-update
  8.0 0.0 reduce-scatter.9.cloned.1.call-start
  8.1 3.1 %collective-permute-start = (bf16[576,1024]{1,0:T(8,128)(2,1)}, bf16[576,1024]{1,0:T(8,128)(2,1)S(1)}, u32[]{:S(2)}, u32[]{:S(2)}) collective-permute-start(bf16[576,1024]{1,0:T(8,128)(2,1)} %bitcast.23), channel_id=1, source_target_pairs={{0,1},{1,2},{2,3},{3,0},{4,5},{5,6},{6,7},{7,4},{8,9},{9,10},{10,1... | collective-permute-start | bytes 3538952 | tf_op jit(solution)/shard_map/ppermute | solution.py:15
  11.2 2.1 collective-permute-start.1
  13.3 43.2 %collective-permute-done = bf16[576,1024]{1,0:T(8,128)(2,1)S(1)} collective-permute-done((bf16[576,1024]{1,0:T(8,128)(2,1)}, bf16[576,1024]{1,0:T(8,128)(2,1)S(1)}, u32[]{:S(2)}, u32[]{:S(2)}) %collective-permute-start) | collective-permute-done | bytes 1179680 | tf_op jit(solution)/shard_map/ppermute | solution.py:15
  56.5 38.5 %collective-permute-start.2 = (bf16[576,1024]{1,0:T(8,128)(2,1)S(1)}, bf16[576,1024]{1,0:T(8,128)(2,1)}, u32[]{:S(2)}, u32[]{:S(2)}) collective-permute-start(bf16[576,1024]{1,0:T(8,128)(2,1)S(1)} %collective-permute-done), channel_id=1, source_target_pairs={{0,1},{1,2},{2,3},{3,0},{4,5},{5,6},{6,7},{7,4},{8,9},{9,10},{10,1... | collective-permute-start | bytes 3538952 | tf_op jit(solution)/shard_map/ppermute | solution.py:15
  94.9 0.6 broadcast_in_dim.10
  95.5 0.0 copy-done.1
  95.6 0.0 copy-start.3
  95.6 0.1 constant_dynamic-update-slice_fusion.3
  95.7 0.1 constant_dynamic-update-slice_fusion.2
  95.8 6.5 %collective-permute-done.1 = bf16[576,1024]{1,0:T(8,128)(2,1)} collective-permute-done((bf16[576,1024]{1,0:T(8,128)(2,1)}, bf16[576,1024]{1,0:T(8,128)(2,1)}, u32[]{:S(2)}, u32[]{:S(2)}) %collective-permute-start.1) | collective-permute-done | bytes 1179680 | tf_op jit(solution)/shard_map/ppermute | solution.py:18
  102.3 1.4 constant_dynamic-update-slice_fusion.1
  103.7 32.6 %collective-permute-done.2 = bf16[576,1024]{1,0:T(8,128)(2,1)} collective-permute-done((bf16[576,1024]{1,0:T(8,128)(2,1)S(1)}, bf16[576,1024]{1,0:T(8,128)(2,1)}, u32[]{:S(2)}, u32[]{:S(2)}) %collective-permute-start.2) | collective-permute-done | bytes 1179680 | tf_op jit(solution)/shard_map/ppermute | solution.py:15
  136.4 1.4 constant_dynamic-update-slice_fusion
  137.8 0.0 copy-done
  137.8 0.0 copy-done.3
  137.8 1.1 fusion.6
  138.9 1.3 collective-permute-start.3
  140.2 1.0 collective-permute-done.3
  141.3 0.0 all-gather.4.cloned.1.call-done
  141.3 4.8 %convolution_bitcast_fusion = f32[2304,96]{1,0:T(8,128)} fusion(bf16[1024,2304]{0,1:T(8,128)(2,1)} %all-gather.4.cloned.1.call-done, bf16[96,1024]{1,0:T(8,128)(2,1)S(1)} %collective-permute-done.3, bf16[192,1024]{1,0:T(8,128)(2,1)S(1)} %bitcast.26, pred[]{:T(512)S(6)} %eq.11), kind=kOutput, calls=%fused_computation.3 | convolution fusion | flops 453083136 | bytes 5996545
  146.1 0.0 reduce-scatter.9.cloned.1.call-update
  146.1 0.0 copy-start.2
  146.1 0.0 reduce-scatter.7.cloned.1.call-start
  146.2 58.4 %all-gather.6.cloned.1.call-done = bf16[1,1024,2304]{1,2,0:T(8,128)(2,1)} async-done(((bf16[1,1024,576]{1,2,0:T(8,128)(2,1)}), bf16[1,1024,2304]{1,2,0:T(8,128)(2,1)}) %all-gather.6.cloned.1.call-update) | async-done | bytes 4718608 | tf_op jit(solution)/shard_map/all_gather | solution.py:40
  204.6 5.2 %fusion.2 = f32[2304,192]{1,0:T(8,128)} fusion(bf16[1024,192]{0,1:T(8,128)(2,1)S(1)} %fusion.6, bf16[1,1024,2304]{1,2,0:T(8,128)(2,1)} %all-gather.6.cloned.1.call-done), kind=kOutput, calls=%fused_computation.2 | convolution fusion | flops 905969664 | bytes 6881280
  209.7 0.0 reduce-scatter.7.cloned.1.call-update
  209.8 25.6 %reduce-scatter.9.cloned.1.call-done = f32[576,96]{1,0:T(8,128)} async-done(((f32[2304,96]{1,0:T(8,128)}), f32[576,96]{1,0:T(8,128)}) %reduce-scatter.9.cloned.1.call-update) | async-done | bytes 221200
  235.3 1.1 copy.10
  236.4 1.6 collective-permute-start.4
  238.0 0.0 copy-done.2
  238.1 37.6 %reduce-scatter.7.cloned.1.call-done = f32[576,192]{1,0:T(8,128)} async-done(((f32[2304,192]{1,0:T(8,128)}), f32[576,192]{1,0:T(8,128)}) %reduce-scatter.7.cloned.1.call-update) | async-done | bytes 442384
  275.6 1.3 copy.8
  276.9 0.0 collective-permute-done.4
  276.9 0.8 fusion.10
  (2 shorter events, 0.0 us)
Async XLA Ops:
  6.5 131.2 %copy-start = (bf16[1,192,2304]{2,1,0:T(8,128)(2,1)S(1)}, bf16[1,192,2304]{2,1,0:T(8,128)(2,1)}, u32[]{:S(2)}) copy-start(bf16[1,192,2304]{2,1,0:T(8,128)(2,1)} %param.6) | copy-start | bytes 2654212
  6.5 89.0 %copy-start.1 = (bf16[1,576,1024]{2,1,0:T(8,128)(2,1)S(1)}, bf16[1,576,1024]{2,1,0:T(8,128)(2,1)}, u32[]{:S(2)}) copy-start(bf16[1,576,1024]{2,1,0:T(8,128)(2,1)} %param.7) | copy-start | bytes 3538948
  6.5 134.7 %all-gather.4.cloned.1.call-start = ((), (), s32[]{:S(2)}) async-start(), calls=%async_computation.2 | async-start | bytes 5308416 | tf_op jit(solution)/shard_map/all_gather | solution.py:48
  7.3 197.3 %all-gather.6.cloned.1.call-start = ((), (), s32[]{:S(2)}) async-start(), calls=%async_computation.3 | async-start | bytes 5898240 | tf_op jit(solution)/shard_map/all_gather | solution.py:40
  8.0 227.3 %reduce-scatter.9.cloned.1.call-start = ((), (), s32[]{:S(2)}) async-start(), calls=%async_computation.5 | async-start | bytes 1474560
  8.1 48.4 %collective-permute-start = (bf16[576,1024]{1,0:T(8,128)(2,1)}, bf16[576,1024]{1,0:T(8,128)(2,1)S(1)}, u32[]{:S(2)}, u32[]{:S(2)}) collective-permute-start(bf16[576,1024]{1,0:T(8,128)(2,1)} %bitcast.23), channel_id=1, source_target_pairs={{0,1},{1,2},{2,3},{3,0},{4,5},{5,6},{6,7},{7,4},{8,9},{9,10},{10,1... | collective-permute-start | bytes 3538952 | tf_op jit(solution)/shard_map/ppermute | solution.py:15
  11.2 91.2 %collective-permute-start.1 = (bf16[576,1024]{1,0:T(8,128)(2,1)}, bf16[576,1024]{1,0:T(8,128)(2,1)}, u32[]{:S(2)}, u32[]{:S(2)}) collective-permute-start(bf16[576,1024]{1,0:T(8,128)(2,1)} %bitcast.24), channel_id=1, source_target_pairs={{0,3},{1,0},{2,1},{3,2},{4,7},{5,4},{6,5},{7,6},{8,11},{9,8},{10,9... | collective-permute-start | bytes 3538952 | tf_op jit(solution)/shard_map/ppermute | solution.py:18
  56.5 79.9 %collective-permute-start.2 = (bf16[576,1024]{1,0:T(8,128)(2,1)S(1)}, bf16[576,1024]{1,0:T(8,128)(2,1)}, u32[]{:S(2)}, u32[]{:S(2)}) collective-permute-start(bf16[576,1024]{1,0:T(8,128)(2,1)S(1)} %collective-permute-done), channel_id=1, source_target_pairs={{0,1},{1,2},{2,3},{3,0},{4,5},{5,6},{6,7},{7,4},{8,9},{9,10},{10,1... | collective-permute-start | bytes 3538952 | tf_op jit(solution)/shard_map/ppermute | solution.py:15
  95.6 42.2 %copy-start.3 = (f32[1,1024]{1,0:T(1,128)S(1)}, f32[1,1024]{1,0:T(1,128)}, u32[]{:S(2)}) copy-start(f32[1,1024]{1,0:T(1,128)} %param.8) | copy-start | bytes 12292
  138.9 2.4 collective-permute-start.3
  146.1 91.9 %copy-start.2 = (f32[1,576]{1,0:T(1,128)S(1)}, f32[1,576]{1,0:T(1,128)}, u32[]{:S(2)}) copy-start(f32[1,576]{1,0:T(1,128)} %param.11) | copy-start | bytes 6916
  146.1 129.5 %reduce-scatter.7.cloned.1.call-start = ((), (), s32[]{:S(2)}) async-start(), calls=%async_computation.4 | async-start | bytes 2949120
  236.4 40.5 %collective-permute-start.4 = (f32[96,576]{1,0:T(8,128)S(1)}, f32[96,576]{1,0:T(8,128)S(1)}, u32[]{:S(2)}, u32[]{:S(2)}) collective-permute-start(f32[96,576]{1,0:T(8,128)S(1)} %copy.10), channel_id=1, source_target_pairs={{0,16},{1,17},{2,18},{3,19},{4,20},{5,21},{6,22},{7,23},{8,24},{9,... | collective-permute-start | bytes 663560 | tf_op jit(solution)/shard_map/ppermute | solution.py:28
Sparse Core Ops, SparseCore 0:
  8.9 89.0 all-gather.3
  99.6 104.9 all-gather.5
  207.5 27.8 reduce-scatter.8
  238.2 37.3 reduce-scatter.6
